TPU v7x, 32 devices: a whole 2x2x4 slice. The times are simulated.
32 devices in a mesh: space: 16 (over z, x, core), tm: 2 (over y).
Axes of the slice: x: 2, y: 2, z: 4, core: 2. Of those that a mesh axis runs over, the one named last changes fastest.
Arguments:
- thermal_anomaly: bfloat16 [128, 140288], P('tm', 'space'), may hold values from -6 to 6
- smoothing_coefs: float32 [128], replicated, may hold values from -0.0075 to 0.0075
Outputs:
- orthonormal_basis: float32 [128, 140288], P(None, ('space', 'tm'))
- triangular_factor: float32 [128, 128], replicated
All inputs are finite; a program needn't handle non-finite values.
Results may differ from a plain program's by a relative error of at most 0.0003.
The roundings to bfloat16 on the way count: a program that leaves them out, or rounds other values in their place, can miss the bound.
Values may be sent and summed in bfloat16 or wider, within the bound.
A program may use at most 64 MiB of HBM per device.

v0:
```python
import functools
import math

import jax
import jax.numpy as jnp
from jax import lax
from jax.experimental import pallas as pl
from jax.experimental.pallas import tpu as pltpu
from jax.sharding import PartitionSpec as P

LANES = 128
SUB = 8
PLANE = 4
CHUNKS = 5
SLABS = 4
GRANT = 16 * 2**20
MESH = pl.DeviceIdType.MESH


def banded(coefficients, rows, cols, delay):
    lag = (
        lax.broadcasted_iota(jnp.int32, (rows, cols), 0)
        + delay
        - lax.broadcasted_iota(jnp.int32, (rows, cols), 1)
    )
    one_hot = lag[:, :, None] == lax.broadcasted_iota(
        jnp.int32, (1, 1, coefficients.shape[0]), 2
    )
    return jnp.sum(jnp.where(one_hot, coefficients.astype(jnp.float32), 0.0), axis=2).astype(
        coefficients.dtype
    )


def general_body(thermal_anomaly, smoothing_coefs):
    steps = thermal_anomaly.shape[0]
    blocks = lax.axis_size("tm")
    coefficients = jnp.concatenate([jnp.ones((1,), jnp.float32), smoothing_coefs]).astype(
        jnp.bfloat16
    )
    reach = min(blocks - 1, -(-(coefficients.shape[0] - 1) // steps))
    record = [thermal_anomaly]
    for distance in range(1, reach + 1):
        route = [(i, i + distance) for i in range(blocks - distance)]
        record.insert(0, lax.ppermute(thermal_anomaly, "tm", route))
    matrix = banded(coefficients, steps, (reach + 1) * steps, reach * steps)
    outgoing = jnp.dot(
        matrix, jnp.concatenate(record, axis=0), preferred_element_type=jnp.float32
    ).astype(jnp.bfloat16)
    arrived = lax.all_to_all(outgoing, "tm", split_axis=1, concat_axis=0, tiled=True)
    gram = lax.psum(
        jnp.dot(arrived, arrived.T, preferred_element_type=jnp.float32), ("space", "tm")
    )
    lower = jnp.linalg.cholesky(gram)
    rows = jax.scipy.linalg.solve_triangular(lower, arrived.astype(jnp.float32), lower=True)
    scale = jnp.sqrt(jnp.float32(thermal_anomaly.shape[1] * lax.axis_size("space")))
    return rows * scale, lower / scale


def place(dst, rows, x_ref, base, start, width, half):
    valid = min(width, half - start)
    low = base + start
    aligned = low // LANES * LANES
    shift = low - aligned
    end = min(aligned + pl.cdiv(shift + valid, LANES) * LANES, x_ref.shape[1])
    value = x_ref[:, aligned:end][:, shift : shift + valid]
    if valid < width:
        edge = valid // LANES * LANES
        dst[rows, start + edge : start + width] = jnp.zeros(
            (value.shape[0], width - edge), dst.dtype
        )
    dst[rows, start : start + valid] = value


def gather_kernel(
    spans,
    x_hbm,
    coef_hbm,
    filtered_hbm,
    gram_ref,
    x_ref,
    coef_ref,
    filtered_ref,
    load_sem,
    store_sem,
    outgoing,
    panel,
    partial,
    pieces,
    reduced,
    planes,
    whole,
    swap_send,
    swap_recv,
    rs_send,
    rs_recv,
    line_send,
    line_recv,
    ag_send,
    ag_recv,
):
    space = lax.axis_index("space")
    tm = lax.axis_index("tm")
    inner = space % PLANE
    plane = space // PLANE
    lines = lax.axis_size("space") // PLANE
    group = PLANE * 2
    me = inner * 2 + tm
    hours = x_ref.shape[0]
    total = 2 * hours
    half = x_ref.shape[1] // 2
    share = total // group

    def in_group(offset):
        other = (me + offset) % group
        return other, (plane * PLANE + other // 2, other % 2)

    def in_line(offset):
        return ((plane + offset) % lines * PLANE + inner, tm)

    barrier = pltpu.get_barrier_semaphore()
    for offset in range(1, group):
        pl.semaphore_signal(barrier, inc=1, device_id=in_group(offset)[1], device_id_type=MESH)
    for offset in range(1, lines):
        pl.semaphore_signal(barrier, inc=1, device_id=in_line(offset), device_id_type=MESH)

    slab = hours // SLABS
    loads = [
        pltpu.make_async_copy(
            x_hbm.at[pl.ds(slab * index, slab)],
            x_ref.at[pl.ds(slab * index, slab)],
            load_sem.at[index],
        )
        for index in range(SLABS)
    ] + [pltpu.make_async_copy(coef_hbm, coef_ref, load_sem.at[SLABS])]
    for copy in loads:
        copy.start()
    for copy in loads:
        copy.wait()

    swaps = []
    for index, (start, width) in enumerate(spans):
        for side in range(2):

            @pl.when(tm == side)
            def _():
                place(outgoing, slice(None), x_ref, (1 - side) * half, start, width, half)

        if index == 0:
            pl.semaphore_wait(barrier, group - 1 + lines - 1)
        copy = pltpu.make_async_remote_copy(
            src_ref=outgoing.at[:, pl.ds(start, width)],
            dst_ref=panel.at[pl.ds(pl.multiple_of(tm * hours, hours), hours), pl.ds(start, width)],
            send_sem=swap_send.at[index],
            recv_sem=swap_recv.at[index],
            device_id=(space, 1 - tm),
            device_id_type=MESH,
        )
        copy.start()
        swaps.append(copy)

    for side in range(2):

        @pl.when(tm == side)
        def _():
            rows = slice(side * hours, (side + 1) * hours)
            for start, width in spans:
                place(panel, rows, x_ref, side * half, start, width, half)

    row = lax.broadcasted_iota(jnp.int32, (total, total), 0)
    col = lax.broadcasted_iota(jnp.int32, (total, total), 1)
    lagged = jnp.broadcast_to(coef_ref[...], (total, total))
    lagged = pltpu.roll(lagged, 1, axis=1, stride=1, stride_axis=0)
    turned = jnp.where(col > row, lagged, jnp.where(col == row, 1.0, 0.0))
    matrix = turned.T.astype(jnp.bfloat16)

    stores = []
    partial[...] = jnp.zeros_like(partial)
    for index, (start, width) in enumerate(spans):
        swaps[index].wait_recv()
        values = jnp.dot(
            matrix, panel[:, start : start + width], preferred_element_type=jnp.float32
        ).astype(jnp.bfloat16)
        filtered_ref[start : start + width, :] = values.T
        store = pltpu.make_async_copy(
            filtered_ref.at[pl.ds(start, width)],
            filtered_hbm.at[pl.ds(start, width)],
            store_sem.at[index],
        )
        store.start()
        stores.append(store)
        partial[...] += lax.dot_general(
            values, values, (((1,), (1,)), ((), ())), preferred_element_type=jnp.float32
        )

    copies = []
    for offset in range(1, group):
        other, device = in_group(offset)
        copy = pltpu.make_async_remote_copy(
            src_ref=partial.at[pl.ds(pl.multiple_of(other * share, share), share)],
            dst_ref=pieces.at[offset - 1],
            send_sem=rs_send.at[offset - 1],
            recv_sem=rs_recv.at[offset - 1],
            device_id=device,
            device_id_type=MESH,
        )
        copy.start()
        copies.append(copy)
    mine = pl.ds(pl.multiple_of(me * share, share), share)
    running = partial[mine, :]
    for offset in range(1, group):
        copies[offset - 1].wait_recv()
        running = running + pieces[offset - 1]
    reduced[...] = running
    planes[plane] = running

    for offset in range(1, lines):
        copy = pltpu.make_async_remote_copy(
            src_ref=reduced,
            dst_ref=planes.at[plane],
            send_sem=line_send.at[offset - 1],
            recv_sem=line_recv.at[offset - 1],
            device_id=in_line(offset),
            device_id_type=MESH,
        )
        copy.start()
        copies.append(copy)
    for offset in range(1, lines):
        copies[group - 1 + offset - 1].wait_recv()
    running = planes[0]
    for index in range(1, lines):
        running = running + planes[index]
    whole[mine, :] = running

    for offset in range(1, group):
        copy = pltpu.make_async_remote_copy(
            src_ref=whole.at[mine],
            dst_ref=whole.at[mine],
            send_sem=ag_send.at[offset - 1],
            recv_sem=ag_recv.at[offset - 1],
            device_id=in_group(offset)[1],
            device_id_type=MESH,
        )
        copy.start()
        copies.append(copy)
    for copy in copies[-(group - 1) :]:
        copy.wait_recv()
    gram_ref[...] = whole[...]
    for copy in swaps + copies:
        copy.wait_send()
    for store in stores:
        store.wait()


def factor(gram_ref, store):
    size = gram_ref.shape[0]
    count = size // SUB
    full = (SUB, size)
    blocks = [gram_ref[SUB * b : SUB * (b + 1), :] for b in range(count)]
    lane = lax.broadcasted_iota(jnp.int32, full, 1)
    sub = lax.broadcasted_iota(jnp.int32, full, 0)
    for b in range(count):
        first = b * SUB
        inside = (lane >= first) & (lane < first + SUB)
        columns = [
            [jnp.broadcast_to(blocks[i][:, first + c : first + c + 1], full) for c in range(SUB)]
            for i in range(b, count)
        ]
        upper = [
            [
                jnp.broadcast_to(columns[0][c][r : r + 1, :], full) if c >= r else None
                for c in range(SUB)
            ]
            for r in range(SUB)
        ]
        rows = [
            jnp.where(
                inside,
                jnp.where(lane == first + r, 1.0, 0.0),
                jnp.broadcast_to(blocks[b][r : r + 1, :], full),
            )
            for r in range(SUB)
        ]
        unit = [[None] * SUB for _ in range(SUB)]
        inverse = [None] * SUB
        for c in range(SUB):
            inverse[c] = 1.0 / upper[c][c]
            for r in range(c + 1, SUB):
                unit[c][r] = upper[c][r] * inverse[c]
                for j in range(r, SUB):
                    upper[r][j] = upper[r][j] - unit[c][r] * upper[c][j]
                rows[r] = rows[r] - unit[c][r] * rows[c]
        store(b, rows, upper, lane, sub)
        solved = [rows[r] * inverse[r] for r in range(SUB)]
        for c in range(SUB - 1, 0, -1):
            for r in range(c):
                solved[r] = solved[r] - unit[r][c] * solved[c]
        for i in range(b + 1, count):
            terms = [columns[i - b][c] * solved[c] for c in range(SUB)]
            while len(terms) > 1:
                terms = [terms[t] + terms[t + 1] for t in range(0, len(terms), 2)]
            blocks[i] = jnp.where(inside, 0.0, blocks[i]) - terms[0]


def basis_kernel(
    points,
    spans,
    gram_ref,
    filtered_hbm,
    basis_hbm,
    factor_hbm,
    filtered_ref,
    basis_ref,
    factor_ref,
    split,
    turned,
    load_sem,
    store_sem,
):
    size = gram_ref.shape[0]
    load = pltpu.make_async_copy(filtered_hbm, filtered_ref, load_sem)
    load.start()
    root = math.sqrt(points)

    def store(b, rows, upper, lane, sub):
        first = b * SUB
        block = rows[0]
        pivot = upper[0][0]
        for r in range(1, SUB):
            block = jnp.where(sub == r, rows[r], block)
            pivot = jnp.where(sub == r, upper[r][r], pivot)
        corner = block
        for r in range(SUB):
            for c in range(r, SUB):
                corner = jnp.where((sub == r) & (lane == first + c), upper[r][c], corner)
        diagonal = jnp.sqrt(pivot)
        here = slice(first, first + SUB)
        inverse = jnp.where(lane <= sub + first, block, 0.0) * (root / diagonal)
        top = inverse.astype(jnp.bfloat16).astype(jnp.float32)
        split[here, :] = top
        split[size + first : size + first + SUB, :] = inverse - top
        turned[here, :] = jnp.where(lane >= sub + first, corner, 0.0) / (diagonal * root)

    factor(gram_ref, store)
    load.wait()
    both_parts = split[...].astype(jnp.bfloat16)
    stores = []
    for index, (start, width) in enumerate(spans):
        rows = pl.ds(start, min(width, basis_ref.shape[0] - start))
        both = lax.dot_general(
            filtered_ref[rows, :],
            both_parts,
            (((1,), (1,)), ((), ())),
            preferred_element_type=jnp.float32,
        )
        basis_ref[rows, :] = both[:, :size] + both[:, size:]
        copy = pltpu.make_async_copy(
            basis_ref.at[rows], basis_hbm.at[rows], store_sem.at[index]
        )
        copy.start()
        stores.append(copy)
        if index == 0:
            factor_ref[...] = turned[...].T
            copy = pltpu.make_async_copy(factor_ref, factor_hbm, store_sem.at[len(spans)])
            copy.start()
            stores.append(copy)
    for copy in stores:
        copy.wait()


def paired_body(thermal_anomaly, smoothing_coefs):
    hours, sites = thermal_anomaly.shape
    total = 2 * hours
    half = sites // 2
    tiles = pl.cdiv(half, LANES)
    edge = max(1, tiles // (2 * CHUNKS))
    step = max(1, pl.cdiv(tiles - 2 * edge, CHUNKS - 2))
    cuts = [0, *range(edge, max(edge, tiles - edge), step), max(edge, tiles - edge), tiles]
    spans = [(a * LANES, (b - a) * LANES) for a, b in zip(cuts, cuts[1:]) if b > a]
    padded = tiles * LANES
    group = PLANE * 2
    lines = lax.axis_size("space") // PLANE
    share = total // group
    dma = pltpu.SemaphoreType.DMA
    vmem = pl.BlockSpec(memory_space=pltpu.VMEM)
    anywhere = pl.BlockSpec(memory_space=pl.ANY)
    filtered, gram = pl.pallas_call(
        functools.partial(gather_kernel, spans),
        out_shape=(
            jax.ShapeDtypeStruct((padded, total), jnp.bfloat16),
            jax.ShapeDtypeStruct((total, total), jnp.float32),
        ),
        in_specs=[pl.BlockSpec(memory_space=pltpu.HBM)] * 2,
        out_specs=(anywhere, vmem),
        scratch_shapes=[
            pltpu.VMEM((hours, sites), jnp.bfloat16),
            pltpu.VMEM((1, total), jnp.float32),
            pltpu.VMEM((padded, total), jnp.bfloat16),
            dma((SLABS + 1,)),
            dma((len(spans),)),
            pltpu.VMEM((hours, padded), jnp.bfloat16),
            pltpu.VMEM((total, padded), jnp.bfloat16),
            pltpu.VMEM((total, total), jnp.float32),
            pltpu.VMEM((group - 1, share, total), jnp.float32),
            pltpu.VMEM((share, total), jnp.float32),
            pltpu.VMEM((lines, share, total), jnp.float32),
            pltpu.VMEM((total, total), jnp.float32),
            dma((len(spans),)),
            dma((len(spans),)),
            dma((group - 1,)),
            dma((group - 1,)),
            dma((lines - 1,)),
            dma((lines - 1,)),
            dma((group - 1,)),
            dma((group - 1,)),
        ],
        compiler_params=pltpu.CompilerParams(
            collective_id=0, has_side_effects=True, vmem_limit_bytes=GRANT
        ),
        name="gather_gram",
    )(thermal_anomaly, smoothing_coefs[: total].reshape(1, total))

    points = sites * lax.axis_size("space")
    basis, lower = pl.pallas_call(
        functools.partial(basis_kernel, points, spans),
        out_shape=(
            jax.ShapeDtypeStruct((half, total), jnp.float32),
            jax.ShapeDtypeStruct((total, total), jnp.float32),
        ),
        in_specs=[vmem, anywhere],
        out_specs=(anywhere, anywhere),
        scratch_shapes=[
            pltpu.VMEM((padded, total), jnp.bfloat16),
            pltpu.VMEM((half, total), jnp.float32),
            pltpu.VMEM((total, total), jnp.float32),
            pltpu.VMEM((2 * total, total), jnp.float32),
            pltpu.VMEM((total, total), jnp.float32),
            dma,
            dma((len(spans) + 1,)),
        ],
        compiler_params=pltpu.CompilerParams(vmem_limit_bytes=GRANT),
        name="factor_basis",
    )(gram, filtered)
    return basis.T, lower


def body(thermal_anomaly, smoothing_coefs):
    hours, sites = thermal_anomaly.shape
    paired = (
        lax.axis_size("tm") == 2
        and 2 * hours == LANES
        and smoothing_coefs.shape[0] >= LANES
        and sites % 2 == 0
        and lax.axis_size("space") % PLANE == 0
        and lax.axis_size("space") > PLANE
    )
    return (paired_body if paired else general_body)(thermal_anomaly, smoothing_coefs)


def solution(mesh):
    placed = (P("tm", "space"), P())
    return jax.shard_map(
        body, mesh=mesh, in_specs=placed, out_specs=(P(None, ("space", "tm")), P()), check_vma=False
    )
```

profile of v0, /device:TPU:0, one launch (start us, length us, event | category | flops | bytes accessed | tf_op | source)
XLA Modules:
  0.0 39.9 jit_solution(13729652790720411013)
XLA Ops:
  0.6 0.0 copy-start
  0.6 1.2 %copy-done = bf16[64,8768]{1,0:T(8,128)(2,1)S(1)} copy-done((bf16[64,8768]{1,0:T(8,128)(2,1)S(1)}, bf16[64,8768]{1,0:T(8,128)(2,1)}, u32[]{:S(2)}) %copy-start) | copy-done | bytes 1122328
  1.9 0.0 copy-start.1
  1.9 0.7 %copy-done.1 = f32[128]{0:T(128)S(1)} copy-done((f32[128]{0:T(128)S(1)}, f32[128]{0:T(128)}, u32[]{:S(2)}) %copy-start.1) | copy-done | bytes 536
  2.5 30.5 %gather_gram.1 = (bf16[4480,128]{1,0:T(8,128)(2,1)S(1)}, f32[128,128]{1,0:T(8,128)S(1)}) custom-call(bf16[64,8768]{1,0:T(8,128)(2,1)S(1)} %copy-done, f32[1,128]{1,0:T(1,128)S(1)} %bitcast.2), custom_call_target="tpu_custom_call" | custom-call | tf_op jit(solution)/shard_map/gather_gram/pallas_call | solution.py:386
  33.1 6.8 %factor_basis.1 = (f32[4384,128]{1,0:T(8,128)}, f32[128,128]{1,0:T(8,128)}) custom-call(f32[128,128]{1,0:T(8,128)S(1)} %get-tuple-element.6.gram_ref, bf16[4480,128]{1,0:T(8,128)(2,1)S(1)} %get-tuple-element.7.filtered_hbm), custom_call_target="tpu_custom_call" | custom-call | tf_op jit(solution)/shard_map/factor_basis/pallas_call | solution.py:423
Async XLA Ops:
  0.6 1.3 %copy-start = (bf16[64,8768]{1,0:T(8,128)(2,1)S(1)}, bf16[64,8768]{1,0:T(8,128)(2,1)}, u32[]{:S(2)}) copy-start(bf16[64,8768]{1,0:T(8,128)(2,1)} %x_hbm.1) | copy-start | bytes 3366916
  1.9 0.7 %copy-start.1 = (f32[128]{0:T(128)S(1)}, f32[128]{0:T(128)}, u32[]{:S(2)}) copy-start(f32[128]{0:T(128)} %param.3) | copy-start | bytes 1540
where the time goes:
time: 40.1 us; the launch traced here: 39.9 us
  Pallas kernels  37.3 us (93%)
  local copies, waits for them, and re-layouts  1.9 us (5%)
  between operations  0.65 us (2%)
    pallas_call x1, Pallas kernels, paired_body(): pl.pallas_call(functools.partial(gather_kernel, spans), out_shape=(jax.Sh...  30.5 us
    pallas_call x1, Pallas kernels, paired_body(): pl.pallas_call(functools.partial(basis_kernel, points, spans), out_shape=...  6.82 us
    unnamed x4, local copies, waits for them, and re-layouts  1.9 us

commit v1 on v0

--- a/solution.py
+++ b/solution.py
@@ -417,7 +417,10 @@
             collective_id=0, has_side_effects=True, vmem_limit_bytes=GRANT
         ),
         name="gather_gram",
-    )(thermal_anomaly, smoothing_coefs[: total].reshape(1, total))
+    )(
+        pltpu.with_memory_space_constraint(thermal_anomaly, pltpu.HBM),
+        pltpu.with_memory_space_constraint(smoothing_coefs[:total].reshape(1, total), pltpu.HBM),
+    )
 
     points = sites * lax.axis_size("space")
     basis, lower = pl.pallas_call(

time: 40.1 us -> 38.3 us (0.955)
  local copies, waits for them, and re-layouts: 1.9 us -> 0 us
    unnamed x4 -> x0, local copies, waits for them, and re-layouts: 1.9 us -> none
where the time goes in v1:
time: 38.3 us; the launch traced here: 38.1 us
  Pallas kernels  37.5 us (98%)
  between operations  0.64 us (2%)
    pallas_call x1, Pallas kernels, paired_body(): pl.pallas_call(functools.partial(gather_kernel, spans), out_shape=(jax.Sh...  30.7 us
    pallas_call x1, Pallas kernels, paired_body(): pl.pallas_call(functools.partial(basis_kernel, points, spans), out_shape=...  6.82 us

profile of v1, /device:TPU:0, one launch (start us, length us, event | category | flops | bytes accessed | tf_op | source)
XLA Modules:
  0.0 38.1 jit_solution(16573419512432196384)
XLA Ops:
  0.6 30.7 %gather_gram.1 = (bf16[4480,128]{1,0:T(8,128)(2,1)S(1)}, f32[128,128]{1,0:T(8,128)S(1)}) custom-call(bf16[64,8768]{1,0:T(8,128)(2,1)} %x_hbm.1, f32[1,128]{1,0:T(1,128)} %bitcast.2), custom_call_target="tpu_custom_call" | custom-call | tf_op jit(solution)/shard_map/gather_gram/pallas_call | solution.py:386
  31.3 6.8 %factor_basis.1 = (f32[4384,128]{1,0:T(8,128)}, f32[128,128]{1,0:T(8,128)}) custom-call(f32[128,128]{1,0:T(8,128)S(1)} %get-tuple-element.6.gram_ref, bf16[4480,128]{1,0:T(8,128)(2,1)S(1)} %get-tuple-element.7.filtered_hbm), custom_call_target="tpu_custom_call" | custom-call | tf_op jit(solution)/shard_map/factor_basis/pallas_call | solution.py:426

commit v2 on v1

v2 whole, which is shorter than its diff:
```python
import functools
import math

import jax
import jax.numpy as jnp
from jax import lax
from jax.experimental import pallas as pl
from jax.experimental.pallas import tpu as pltpu
from jax.sharding import PartitionSpec as P

LANES = 128
SUB = 8
PLANE = 4
CHUNKS = 5
FIRST = 17 * LANES
FAR_FIRST = (7, 5, 3, 1, 6, 4, 2)
LINE_AFTER = 0
GATHER_AFTER = 1
SPLIT = 4
GRANT = 16 * 2**20
MESH = pl.DeviceIdType.MESH


def banded(coefficients, rows, cols, delay):
    lag = (
        lax.broadcasted_iota(jnp.int32, (rows, cols), 0)
        + delay
        - lax.broadcasted_iota(jnp.int32, (rows, cols), 1)
    )
    one_hot = lag[:, :, None] == lax.broadcasted_iota(
        jnp.int32, (1, 1, coefficients.shape[0]), 2
    )
    return jnp.sum(jnp.where(one_hot, coefficients.astype(jnp.float32), 0.0), axis=2).astype(
        coefficients.dtype
    )


def general_body(thermal_anomaly, smoothing_coefs):
    steps = thermal_anomaly.shape[0]
    blocks = lax.axis_size("tm")
    coefficients = jnp.concatenate([jnp.ones((1,), jnp.float32), smoothing_coefs]).astype(
        jnp.bfloat16
    )
    reach = min(blocks - 1, -(-(coefficients.shape[0] - 1) // steps))
    record = [thermal_anomaly]
    for distance in range(1, reach + 1):
        route = [(i, i + distance) for i in range(blocks - distance)]
        record.insert(0, lax.ppermute(thermal_anomaly, "tm", route))
    matrix = banded(coefficients, steps, (reach + 1) * steps, reach * steps)
    outgoing = jnp.dot(
        matrix, jnp.concatenate(record, axis=0), preferred_element_type=jnp.float32
    ).astype(jnp.bfloat16)
    arrived = lax.all_to_all(outgoing, "tm", split_axis=1, concat_axis=0, tiled=True)
    gram = lax.psum(
        jnp.dot(arrived, arrived.T, preferred_element_type=jnp.float32), ("space", "tm")
    )
    lower = jnp.linalg.cholesky(gram)
    rows = jax.scipy.linalg.solve_triangular(lower, arrived.astype(jnp.float32), lower=True)
    scale = jnp.sqrt(jnp.float32(thermal_anomaly.shape[1] * lax.axis_size("space")))
    return rows * scale, lower / scale


def gather_kernel(
    spans,
    x_hbm,
    coef_hbm,
    filtered_ref,
    late_ref,
    early_ref,
    x_ref,
    coef_ref,
    tail,
    panel,
    partial,
    pieces,
    reduced,
    planes,
    first_partial,
    first_pieces,
    first_reduced,
    first_planes,
    first_whole,
    whole,
    load_sem,
    swap_send,
    swap_recv,
    rs_send,
    rs_recv,
    line_send,
    line_recv,
    ag_send,
    ag_recv,
    first_rs_send,
    first_rs_recv,
    first_line_send,
    first_line_recv,
    first_ag_send,
    first_ag_recv,
):
    space = lax.axis_index("space")
    tm = lax.axis_index("tm")
    inner = space % PLANE
    plane = space // PLANE
    lines = lax.axis_size("space") // PLANE
    group = PLANE * 2
    me = inner * 2 + tm
    hours, sites = x_ref.shape
    total = 2 * hours
    half = sites // 2
    low = half // LANES * LANES
    shift = half - low
    full = panel.shape[1] - LANES
    share = hours // group
    quarter = first_partial.shape[0] // PLANE

    def in_group(k):
        x = inner // 2
        core = inner % 2
        x = 1 - x if k & 4 else x
        core = 1 - core if k & 2 else core
        side = 1 - tm if k & 1 else tm
        near = x * 2 + core
        return near * 2 + side, (plane * PLANE + near, side)

    def in_line(offset):
        return ((plane + offset) % lines * PLANE + inner, tm)

    barrier = pltpu.get_barrier_semaphore()
    for offset in range(1, lines):
        pl.semaphore_signal(barrier, inc=1, device_id=in_line(offset), device_id_type=MESH)
    for k in FAR_FIRST:
        pl.semaphore_signal(barrier, inc=1, device_id=in_group(k)[1], device_id_type=MESH)

    own = pl.ds(pl.multiple_of(tm * hours, hours), hours)
    load_x = pltpu.make_async_copy(x_hbm, x_ref, load_sem.at[0])
    load_coef = pltpu.make_async_copy(coef_hbm, coef_ref, load_sem.at[1])
    load_own = pltpu.make_async_copy(
        x_hbm.at[:, pl.ds(pl.multiple_of(tm * low, LANES), full)],
        panel.at[own, pl.ds(0, full)],
        load_sem.at[2],
    )
    for copy in (load_x, load_coef, load_own):
        copy.start()

    pl.semaphore_wait(barrier, group - 1 + lines - 1)
    swaps = []
    for index, (start, width) in enumerate(spans):
        copy = pltpu.make_async_remote_copy(
            src_ref=x_hbm.at[
                :, pl.ds(pl.multiple_of((1 - tm) * low + start, LANES), width)
            ],
            dst_ref=panel.at[own, pl.ds(start, width)],
            send_sem=swap_send.at[index],
            recv_sem=swap_recv.at[index],
            device_id=(space, 1 - tm),
            device_id_type=MESH,
        )
        swaps.append(copy)
    for copy in swaps[:-1]:
        copy.start()

    load_x.wait()
    for side in range(2):

        @pl.when(tm == side)
        def _():
            for target, to in ((tail, 1 - side), (None, side)):
                begin = to * low + full
                width = min(LANES, sites - begin)
                value = x_ref[:, begin : begin + width]
                if width < LANES:
                    pad = jnp.zeros((hours, LANES - width), value.dtype)
                    value = jnp.concatenate([value, pad], axis=1)
                if target is None:
                    panel[side * hours : (side + 1) * hours, full : full + LANES] = value
                else:
                    target[...] = value

    tail_copy = pltpu.make_async_remote_copy(
        src_ref=tail,
        dst_ref=panel.at[own, pl.ds(full, LANES)],
        send_sem=swap_send.at[len(spans)],
        recv_sem=swap_recv.at[len(spans)],
        device_id=(space, 1 - tm),
        device_id_type=MESH,
    )
    tail_copy.start()
    swaps[-1].start()

    load_coef.wait()
    row = lax.broadcasted_iota(jnp.int32, (total, total), 0)
    col = lax.broadcasted_iota(jnp.int32, (total, total), 1)
    lagged = jnp.broadcast_to(coef_ref[...], (total, total))
    lagged = pltpu.roll(lagged, 1, axis=1, stride=1, stride_axis=0)
    turned = jnp.where(col > row, lagged, jnp.where(col == row, 1.0, 0.0))
    matrix = turned.T.astype(jnp.bfloat16)
    corner = matrix[:hours, :hours]

    def first_near(offset):
        near = (inner + offset) % PLANE
        return near, plane * PLANE + near

    def first_scatter(offset):
        near, other = first_near(offset)
        return pltpu.make_async_remote_copy(
            src_ref=first_partial.at[pl.ds(pl.multiple_of(near * quarter, quarter), quarter)],
            dst_ref=first_pieces.at[offset - 1],
            send_sem=first_rs_send.at[offset - 1],
            recv_sem=first_rs_recv.at[offset - 1],
            device_id=(other, tm),
            device_id_type=MESH,
        )

    def first_line(offset):
        return pltpu.make_async_remote_copy(
            src_ref=first_reduced,
            dst_ref=first_planes.at[plane],
            send_sem=first_line_send.at[offset - 1],
            recv_sem=first_line_recv.at[offset - 1],
            device_id=in_line(offset),
            device_id_type=MESH,
        )

    first_mine = pl.ds(pl.multiple_of(inner * quarter, quarter), quarter)

    def first_gather(offset, side):
        return pltpu.make_async_remote_copy(
            src_ref=first_whole.at[first_mine],
            dst_ref=first_whole.at[first_mine],
            send_sem=first_ag_send.at[side * PLANE + offset],
            recv_sem=first_ag_recv.at[offset],
            device_id=(first_near(offset)[1], side),
            device_id_type=MESH,
        )

    @pl.when(tm == 0)
    def _():
        gram = jnp.zeros((hours, hours), jnp.float32)
        cuts = [*range(0, low + full, FIRST), low + full]
        parts = [x_ref[:, a:b] for a, b in zip(cuts, cuts[1:])] + [tail[...]]
        for part in parts:
            values = jnp.dot(corner, part, preferred_element_type=jnp.float32).astype(jnp.bfloat16)
            gram = gram + lax.dot_general(
                values, values, (((1,), (1,)), ((), ())), preferred_element_type=jnp.float32
            )
        first_partial[...] = jnp.concatenate([gram[: hours // 2], gram[hours // 2 :]], axis=1)
        for offset in range(1, PLANE):
            first_scatter(offset).start()

    def first_stage_line():
        @pl.when(tm == 0)
        def _():
            running = first_partial[first_mine, :]
            for offset in range(1, PLANE):
                first_scatter(offset).wait_recv()
                running = running + first_pieces[offset - 1]
            first_reduced[...] = running
            first_planes[plane] = running
            for offset in range(1, lines):
                first_line(offset).start()

    def first_stage_gather():
        @pl.when(tm == 0)
        def _():
            for offset in range(1, lines):
                first_line(offset).wait_recv()
            running = first_planes[0]
            for index in range(1, lines):
                running = running + first_planes[index]
            first_whole[first_mine, :] = running
            for side in (1, 0):
                for offset in range(PLANE):
                    if side or offset:
                        first_gather(offset, side).start()

    load_own.wait()
    partial[...] = jnp.zeros_like(partial)
    for index, (start, width) in enumerate(spans):
        swaps[index].wait_recv()
        if index == len(spans) - 1:
            tail_copy.wait_recv()
            width += LANES
        values = jnp.dot(
            matrix, panel[:, start : start + width], preferred_element_type=jnp.float32
        )
        if start < shift or start + width > half:
            point = lax.broadcasted_iota(jnp.int32, (total, width), 1) + (start - tm * shift)
            values = jnp.where((point >= 0) & (point < half), values, 0.0)
        values = values.astype(jnp.bfloat16)
        filtered_ref[start : start + width, :] = values.T
        partial[...] += lax.dot_general(
            values[hours:], values, (((1,), (1,)), ((), ())), preferred_element_type=jnp.float32
        )
        if index == min(LINE_AFTER, len(spans) - 2):
            first_stage_line()
        if index == min(GATHER_AFTER, len(spans) - 2):
            first_stage_gather()

    copies = []
    for k in FAR_FIRST:
        other, device = in_group(k)
        copy = pltpu.make_async_remote_copy(
            src_ref=partial.at[pl.ds(pl.multiple_of(other * share, share), share)],
            dst_ref=pieces.at[k - 1],
            send_sem=rs_send.at[k - 1],
            recv_sem=rs_recv.at[k - 1],
            device_id=device,
            device_id_type=MESH,
        )
        copy.start()
        copies.append(copy)

    @pl.when(tm == 0)
    def _():
        for offset in range(1, PLANE):
            first_gather(offset, 0).wait_recv()

    @pl.when(tm == 1)
    def _():
        for offset in range(PLANE):
            first_gather(offset, 1).wait_recv()

    blank = jnp.zeros((SUB, hours), jnp.float32)
    blocks = []
    for b in range(hours // SUB):
        begin = b * SUB
        packed = first_whole[begin % (hours // 2) : begin % (hours // 2) + SUB, :]
        side = begin // (hours // 2)
        blocks.append(
            jnp.concatenate([packed[:, side * hours : (side + 1) * hours], blank], axis=1)
        )

    def store(first, rows, upper, lane, sub):
        block, pivot, corner = assemble(first, rows, upper, lane, sub)
        diagonal = jnp.sqrt(pivot)
        early_ref[first : first + SUB, :] = (
            jnp.where(lane <= sub + first, block, 0.0) / diagonal
        )
        early_ref[hours + first : hours + first + SUB, :] = (
            jnp.where(lane >= sub + first, corner, 0.0) / diagonal
        )

    for b in range(SPLIT):
        eliminate(blocks, b, 0, store)

    mine = pl.ds(pl.multiple_of(me * share, share), share)
    running = partial[mine, :]
    for k, copy in zip(FAR_FIRST, copies):
        copy.wait_recv()
        running = running + pieces[k - 1]
    reduced[...] = running
    planes[plane] = running

    for offset in range(1, lines):
        copy = pltpu.make_async_remote_copy(
            src_ref=reduced,
            dst_ref=planes.at[plane],
            send_sem=line_send.at[offset - 1],
            recv_sem=line_recv.at[offset - 1],
            device_id=in_line(offset),
            device_id_type=MESH,
        )
        copy.start()
        copies.append(copy)
    for b in range(SPLIT, len(blocks)):
        eliminate(blocks, b, 0, store)
    for copy in copies[group - 1 :]:
        copy.wait_recv()
    running = planes[0]
    for index in range(1, lines):
        running = running + planes[index]
    whole[mine, :] = running

    for k in FAR_FIRST:
        copy = pltpu.make_async_remote_copy(
            src_ref=whole.at[mine],
            dst_ref=whole.at[mine],
            send_sem=ag_send.at[k - 1],
            recv_sem=ag_recv.at[k - 1],
            device_id=in_group(k)[1],
            device_id_type=MESH,
        )
        copy.start()
        copies.append(copy)
    for copy in swaps + [tail_copy] + copies[: -(group - 1)]:
        copy.wait_send()

    @pl.when(tm == 0)
    def _():
        for offset in range(1, PLANE):
            first_scatter(offset).wait_send()
        for offset in range(1, lines):
            first_line(offset).wait_send()
        for side in (1, 0):
            for offset in range(PLANE):
                if side or offset:
                    first_gather(offset, side).wait_send()

    for copy in copies[-(group - 1) :]:
        copy.wait_recv()
    late_ref[...] = whole[...]
    for copy in copies[-(group - 1) :]:
        copy.wait_send()


def assemble(first, rows, upper, lane, sub):
    block = rows[0]
    pivot = upper[0][0]
    for r in range(1, SUB):
        block = jnp.where(sub == r, rows[r], block)
        pivot = jnp.where(sub == r, upper[r][r], pivot)
    corner = block
    for r in range(SUB):
        for c in range(r, SUB):
            corner = jnp.where((sub == r) & (lane == first + c), upper[r][c], corner)
    return block, pivot, corner


def eliminate(blocks, b, origin, store):
    count = len(blocks)
    full = blocks[0].shape
    lane = lax.broadcasted_iota(jnp.int32, full, 1)
    sub = lax.broadcasted_iota(jnp.int32, full, 0)
    first = origin + b * SUB
    inside = (lane >= first) & (lane < first + SUB)
    columns = [
        [jnp.broadcast_to(blocks[i][:, first + c : first + c + 1], full) for c in range(SUB)]
        for i in range(b, count)
    ]
    upper = [
        [
            jnp.broadcast_to(columns[0][c][r : r + 1, :], full) if c >= r else None
            for c in range(SUB)
        ]
        for r in range(SUB)
    ]
    rows = [
        jnp.where(
            inside,
            jnp.where(lane == first + r, 1.0, 0.0),
            jnp.broadcast_to(blocks[b][r : r + 1, :], full),
        )
        for r in range(SUB)
    ]
    unit = [[None] * SUB for _ in range(SUB)]
    inverse = [None] * SUB
    for c in range(SUB):
        inverse[c] = 1.0 / upper[c][c]
        for r in range(c + 1, SUB):
            unit[c][r] = upper[c][r] * inverse[c]
            for j in range(r, SUB):
                upper[r][j] = upper[r][j] - unit[c][r] * upper[c][j]
            rows[r] = rows[r] - unit[c][r] * rows[c]
    store(first, rows, upper, lane, sub)
    solved = [rows[r] * inverse[r] for r in range(SUB)]
    for c in range(SUB - 1, 0, -1):
        for r in range(c):
            solved[r] = solved[r] - unit[r][c] * solved[c]
    for i in range(b + 1, count):
        terms = [columns[i - b][c] * solved[c] for c in range(SUB)]
        while len(terms) > 1:
            terms = [terms[t] + terms[t + 1] for t in range(0, len(terms), 2)]
        blocks[i] = jnp.where(inside, 0.0, blocks[i]) - terms[0]


def exact(a, b, dims):
    return lax.dot_general(
        a,
        b,
        (dims, ((), ())),
        precision=lax.Precision.HIGHEST,
        preferred_element_type=jnp.float32,
    )


def basis_kernel(
    points,
    shift,
    spans,
    late_ref,
    early_ref,
    filtered_ref,
    basis_hbm,
    factor_hbm,
    basis_ref,
    factor_ref,
    split,
    turned,
    store_sem,
):
    hours, size = late_ref.shape
    root = math.sqrt(points)
    late = late_ref[...]
    head = early_ref[:hours, :]
    lane = lax.broadcasted_iota(jnp.int32, (hours, size), 1)
    left = lane < hours
    below = exact(late, head, ((1,), (1,)))
    padded = jnp.concatenate([jnp.zeros_like(late), late], axis=0)
    across = jnp.where(left, 0.0, exact(head, padded, ((1,), (1,))))
    state = jnp.where(left, 0.0, late) - exact(below, head + across, ((1,), (0,)))

    def halves(here, inverse):
        begin, end = here
        top = inverse.astype(jnp.bfloat16).astype(jnp.float32)
        split[begin:end, :] = top
        split[size + begin : size + end, :] = inverse - top

    halves((0, hours), head * root)
    turned[:hours, :] = (early_ref[hours:, :] + across) / root

    def store(first, rows, upper, lane, sub):
        block, pivot, corner = assemble(first, rows, upper, lane, sub)
        diagonal = jnp.sqrt(pivot)
        inverse = jnp.where(lane <= sub + first, block, 0.0) * (root / diagonal)
        halves((first, first + SUB), inverse)
        turned[first : first + SUB, :] = jnp.where(lane >= sub + first, corner, 0.0) / (
            diagonal * root
        )

    blocks = [state[SUB * b : SUB * (b + 1), :] for b in range(hours // SUB)]
    for b in range(len(blocks)):
        eliminate(blocks, b, hours, store)
    both_parts = split[...].astype(jnp.bfloat16)
    offset = lax.axis_index("tm") * shift
    stores = []
    for index, (start, width) in enumerate(spans):
        width = min(width, basis_ref.shape[0] - start)
        both = lax.dot_general(
            filtered_ref[pl.ds(pl.multiple_of(offset + start, 2 * SUB), width), :],
            both_parts,
            (((1,), (1,)), ((), ())),
            preferred_element_type=jnp.float32,
        )
        rows = pl.ds(start, width)
        basis_ref[rows, :] = both[:, :size] + both[:, size:]
        copy = pltpu.make_async_copy(
            basis_ref.at[rows], basis_hbm.at[rows], store_sem.at[index]
        )
        copy.start()
        stores.append(copy)
        if index == 0:
            factor_ref[...] = turned[...].T
            copy = pltpu.make_async_copy(factor_ref, factor_hbm, store_sem.at[len(spans)])
            copy.start()
            stores.append(copy)
    for copy in stores:
        copy.wait()


def cut(tiles):
    edge = max(1, tiles // (2 * CHUNKS))
    step = max(1, pl.cdiv(tiles - 2 * edge, CHUNKS - 2))
    cuts = [0, *range(edge, max(edge, tiles - edge), step), max(edge, tiles - edge), tiles]
    return [(a * LANES, (b - a) * LANES) for a, b in zip(cuts, cuts[1:]) if b > a]


def paired_body(thermal_anomaly, smoothing_coefs):
    hours, sites = thermal_anomaly.shape
    total = 2 * hours
    half = sites // 2
    shift = half % LANES
    tiles = pl.cdiv(shift + half, LANES)
    swap_spans = cut(tiles - 1)
    padded = tiles * LANES
    group = PLANE * 2
    lines = lax.axis_size("space") // PLANE
    share = hours // group
    quarter = hours // 2 // PLANE
    dma = pltpu.SemaphoreType.DMA
    vmem = pl.BlockSpec(memory_space=pltpu.VMEM)
    anywhere = pl.BlockSpec(memory_space=pl.ANY)
    filtered, late, early = pl.pallas_call(
        functools.partial(gather_kernel, swap_spans),
        out_shape=(
            jax.ShapeDtypeStruct((padded, total), jnp.bfloat16),
            jax.ShapeDtypeStruct((hours, total), jnp.float32),
            jax.ShapeDtypeStruct((total, total), jnp.float32),
        ),
        in_specs=[pl.BlockSpec(memory_space=pltpu.HBM)] * 2,
        out_specs=(vmem, vmem, vmem),
        scratch_shapes=[
            pltpu.VMEM((hours, sites), jnp.bfloat16),
            pltpu.VMEM((1, total), jnp.float32),
            pltpu.VMEM((hours, LANES), jnp.bfloat16),
            pltpu.VMEM((total, padded), jnp.bfloat16),
            pltpu.VMEM((hours, total), jnp.float32),
            pltpu.VMEM((group - 1, share, total), jnp.float32),
            pltpu.VMEM((share, total), jnp.float32),
            pltpu.VMEM((lines, share, total), jnp.float32),
            pltpu.VMEM((hours // 2, total), jnp.float32),
            pltpu.VMEM((PLANE - 1, quarter, total), jnp.float32),
            pltpu.VMEM((quarter, total), jnp.float32),
            pltpu.VMEM((lines, quarter, total), jnp.float32),
            pltpu.VMEM((hours // 2, total), jnp.float32),
            pltpu.VMEM((hours, total), jnp.float32),
            dma((3,)),
            dma((len(swap_spans) + 1,)),
            dma((len(swap_spans) + 1,)),
            dma((group - 1,)),
            dma((group - 1,)),
            dma((lines - 1,)),
            dma((lines - 1,)),
            dma((group - 1,)),
            dma((group - 1,)),
            dma((PLANE - 1,)),
            dma((PLANE - 1,)),
            dma((lines - 1,)),
            dma((lines - 1,)),
            dma((group,)),
            dma((PLANE,)),
        ],
        compiler_params=pltpu.CompilerParams(
            collective_id=0, has_side_effects=True, vmem_limit_bytes=GRANT
        ),
        name="gather_gram",
    )(
        pltpu.with_memory_space_constraint(thermal_anomaly, pltpu.HBM),
        pltpu.with_memory_space_constraint(smoothing_coefs[:total].reshape(1, total), pltpu.HBM),
    )

    points = sites * lax.axis_size("space")
    spans = cut(pl.cdiv(half, LANES))
    basis, lower = pl.pallas_call(
        functools.partial(basis_kernel, points, shift, spans),
        out_shape=(
            jax.ShapeDtypeStruct((half, total), jnp.float32),
            jax.ShapeDtypeStruct((total, total), jnp.float32),
        ),
        in_specs=[vmem, vmem, vmem],
        out_specs=(anywhere, anywhere),
        scratch_shapes=[
            pltpu.VMEM((half, total), jnp.float32),
            pltpu.VMEM((total, total), jnp.float32),
            pltpu.VMEM((2 * total, total), jnp.float32),
            pltpu.VMEM((total, total), jnp.float32),
            dma((len(spans) + 1,)),
        ],
        compiler_params=pltpu.CompilerParams(vmem_limit_bytes=GRANT),
        name="factor_basis",
    )(late, early, filtered)
    return basis.T, lower


def body(thermal_anomaly, smoothing_coefs):
    hours, sites = thermal_anomaly.shape
    paired = (
        lax.axis_size("tm") == 2
        and 2 * hours == LANES
        and smoothing_coefs.shape[0] >= LANES
        and sites % 2 == 0
        and sites // 2 % LANES % (2 * SUB) == 0
        and sites // 2 > 8 * LANES
        and lax.axis_size("space") % PLANE == 0
        and lax.axis_size("space") > PLANE
    )
    return (paired_body if paired else general_body)(thermal_anomaly, smoothing_coefs)


def solution(mesh):
    placed = (P("tm", "space"), P())
    return jax.shard_map(
        body, mesh=mesh, in_specs=placed, out_specs=(P(None, ("space", "tm")), P()), check_vma=False
    )
```

time: 38.3 us -> 36.1 us (0.943)
  Pallas kernels: 37.5 us -> 35.3 us
    pallas_call x2, Pallas kernels: 37.5 us -> 35.3 us  [the longest x1 30.9 us: paired_body(): pl.pallas_call(functools.partial(gather_kernel, swap_spans), out_shape=(j...]
where the time goes in v2:
time: 36.1 us; the launch traced here: 36 us
  Pallas kernels  35.3 us (98%)
  between operations  0.64 us (2%)
    pallas_call x1, Pallas kernels, paired_body(): pl.pallas_call(functools.partial(gather_kernel, swap_spans), out_shape=(j...  30.9 us
    pallas_call x1, Pallas kernels, paired_body(): pl.pallas_call(functools.partial(basis_kernel, points, shift, spans), out...  4.45 us

profile of v2, /device:TPU:0, one launch (start us, length us, event | category | flops | bytes accessed | tf_op | source)
XLA Modules:
  0.0 36.0 jit_solution(11648232229995055242)
XLA Ops:
  0.6 30.9 %gather_gram.1 = (bf16[4480,128]{1,0:T(8,128)(2,1)S(1)}, f32[64,128]{1,0:T(8,128)S(1)}, f32[128,128]{1,0:T(8,128)S(1)}) custom-call(bf16[64,8768]{1,0:T(8,128)(2,1)} %x_hbm.1, f32[1,128]{1,0:T(1,128)} %bitcast.2), custom_call_target="tpu_custom_call" | custom-call | tf_op jit(solution)/shard_map/gather_gram/pallas_call | solution.py:572
  31.5 4.5 %factor_basis.1 = (f32[4384,128]{1,0:T(8,128)}, f32[128,128]{1,0:T(8,128)}) custom-call(f32[64,128]{1,0:T(8,128)S(1)} %get-tuple-element.7.late_ref, f32[128,128]{1,0:T(8,128)S(1)} %get-tuple-element.8.early_ref, bf16[4480,128]{1,0:T(8,128)(2,1)S(1)} %get-tuple-element.9.filtered_ref), custom_call_target="tpu_custom_call" | custom-call | tf_op jit(solution)/shard_map/factor_basis/pallas_call | solution.py:623

commit v3 on v2

--- a/solution.py
+++ b/solution.py
@@ -14,6 +14,7 @@
 CHUNKS = 5
 FIRST = 17 * LANES
 FAR_FIRST = (7, 5, 3, 1, 6, 4, 2)
+NEXT = (1, 4, 2)
 LINE_AFTER = 0
 GATHER_AFTER = 1
 SPLIT = 4
@@ -96,6 +97,9 @@
     first_line_recv,
     first_ag_send,
     first_ag_recv,
+    mate_sem,
+    across_sem,
+    along_sem,
 ):
     space = lax.axis_index("space")
     tm = lax.axis_index("tm")
@@ -126,10 +130,23 @@
         return ((plane + offset) % lines * PLANE + inner, tm)
 
     barrier = pltpu.get_barrier_semaphore()
-    for offset in range(1, lines):
-        pl.semaphore_signal(barrier, inc=1, device_id=in_line(offset), device_id_type=MESH)
-    for k in FAR_FIRST:
+    for k in NEXT:
         pl.semaphore_signal(barrier, inc=1, device_id=in_group(k)[1], device_id_type=MESH)
+
+    def tell_line(semaphore):
+        for step, there in ((-1, plane > 0), (1, plane < lines - 1)):
+
+            @pl.when(there)
+            def _():
+                pl.semaphore_signal(
+                    semaphore,
+                    inc=1,
+                    device_id=(space + step * PLANE, tm),
+                    device_id_type=MESH,
+                )
+
+    tell_line(barrier)
+    beside = (plane + lines - 1) // lines + (2 * lines - 2 - plane) // lines
 
     own = pl.ds(pl.multiple_of(tm * hours, hours), hours)
     load_x = pltpu.make_async_copy(x_hbm, x_ref, load_sem.at[0])
@@ -142,7 +159,7 @@
     for copy in (load_x, load_coef, load_own):
         copy.start()
 
-    pl.semaphore_wait(barrier, group - 1 + lines - 1)
+    pl.semaphore_wait(barrier, len(NEXT) + beside)
     swaps = []
     for index, (start, width) in enumerate(spans):
         copy = pltpu.make_async_remote_copy(
@@ -158,6 +175,13 @@
         swaps.append(copy)
     for copy in swaps[:-1]:
         copy.start()
+    pl.semaphore_signal(mate_sem, inc=1, device_id=in_group(2)[1], device_id_type=MESH)
+    pl.semaphore_wait(mate_sem, 1)
+    pl.semaphore_signal(across_sem, inc=1, device_id=in_group(4)[1], device_id_type=MESH)
+    for reach in range(lines - 2):
+        if reach:
+            pl.semaphore_wait(along_sem.at[reach - 1], beside)
+        tell_line(along_sem.at[reach])
 
     load_x.wait()
     for side in range(2):
@@ -273,6 +297,8 @@
                     if side or offset:
                         first_gather(offset, side).start()
 
+    pl.semaphore_wait(across_sem, 1)
+    pl.semaphore_wait(along_sem.at[lines - 3], beside)
     load_own.wait()
     partial[...] = jnp.zeros_like(partial)
     for index, (start, width) in enumerate(spans):
@@ -287,7 +313,8 @@
             point = lax.broadcasted_iota(jnp.int32, (total, width), 1) + (start - tm * shift)
             values = jnp.where((point >= 0) & (point < half), values, 0.0)
         values = values.astype(jnp.bfloat16)
-        filtered_ref[start : start + width, :] = values.T
+        if index < len(spans) - 1:
+            filtered_ref[start : start + width, :] = values.T
         partial[...] += lax.dot_general(
             values[hours:], values, (((1,), (1,)), ((), ())), preferred_element_type=jnp.float32
         )
@@ -309,6 +336,7 @@
         )
         copy.start()
         copies.append(copy)
+    filtered_ref[start : start + width, :] = values.T
 
     @pl.when(tm == 0)
     def _():
@@ -444,6 +472,7 @@
     ]
     unit = [[None] * SUB for _ in range(SUB)]
     inverse = [None] * SUB
+    solved = [None] * SUB
     for c in range(SUB):
         inverse[c] = 1.0 / upper[c][c]
         for r in range(c + 1, SUB):
@@ -451,11 +480,12 @@
             for j in range(r, SUB):
                 upper[r][j] = upper[r][j] - unit[c][r] * upper[c][j]
             rows[r] = rows[r] - unit[c][r] * rows[c]
-    store(first, rows, upper, lane, sub)
-    solved = [rows[r] * inverse[r] for r in range(SUB)]
-    for c in range(SUB - 1, 0, -1):
+        solved[c] = rows[c] * inverse[c]
         for r in range(c):
             solved[r] = solved[r] - unit[r][c] * solved[c]
+            for j in range(c + 1, SUB):
+                unit[r][j] = unit[r][j] - unit[r][c] * unit[c][j]
+    store(first, rows, upper, lane, sub)
     for i in range(b + 1, count):
         terms = [columns[i - b][c] * solved[c] for c in range(SUB)]
         while len(terms) > 1:
@@ -608,6 +638,9 @@
             dma((lines - 1,)),
             dma((group,)),
             dma((PLANE,)),
+            pltpu.SemaphoreType.REGULAR,
+            pltpu.SemaphoreType.REGULAR,
+            pltpu.SemaphoreType.REGULAR((lines - 2,)),
         ],
         compiler_params=pltpu.CompilerParams(
             collective_id=0, has_side_effects=True, vmem_limit_bytes=GRANT
@@ -651,7 +684,7 @@
         and sites // 2 % LANES % (2 * SUB) == 0
         and sites // 2 > 8 * LANES
         and lax.axis_size("space") % PLANE == 0
-        and lax.axis_size("space") > PLANE
+        and lax.axis_size("space") > 2 * PLANE
     )
     return (paired_body if paired else general_body)(thermal_anomaly, smoothing_coefs)
 

time: 36.1 us -> 35.2 us (0.975)
  Pallas kernels: 35.3 us -> 34.4 us
    pallas_call x1, Pallas kernels: 30.9 us -> 30 us  [paired_body(): pl.pallas_call(functools.partial(gather_kernel, swap_spans), out_shape=(j...]
where the time goes in v3:
time: 35.2 us; the launch traced here: 35 us
  Pallas kernels  34.4 us (98%)
  between operations  0.64 us (2%)
    pallas_call x1, Pallas kernels, paired_body(): pl.pallas_call(functools.partial(gather_kernel, swap_spans), out_shape=(j...  30 us
    pallas_call x1, Pallas kernels, paired_body(): pl.pallas_call(functools.partial(basis_kernel, points, shift, spans), out...  4.4 us

profile of v3, /device:TPU:0, one launch (start us, length us, event | category | flops | bytes accessed | tf_op | source)
XLA Modules:
  0.0 35.0 jit_solution(10451286421345674047)
XLA Ops:
  0.6 30.0 %gather_gram.1 = (bf16[4480,128]{1,0:T(8,128)(2,1)S(1)}, f32[64,128]{1,0:T(8,128)S(1)}, f32[128,128]{1,0:T(8,128)S(1)}) custom-call(bf16[64,8768]{1,0:T(8,128)(2,1)} %x_hbm.1, f32[1,128]{1,0:T(1,128)} %bitcast.2), custom_call_target="tpu_custom_call" | custom-call | tf_op jit(solution)/shard_map/gather_gram/pallas_call | solution.py:602
  30.6 4.4 %factor_basis.1 = (f32[4384,128]{1,0:T(8,128)}, f32[128,128]{1,0:T(8,128)}) custom-call(f32[64,128]{1,0:T(8,128)S(1)} %get-tuple-element.7.late_ref, f32[128,128]{1,0:T(8,128)S(1)} %get-tuple-element.8.early_ref, bf16[4480,128]{1,0:T(8,128)(2,1)S(1)} %get-tuple-element.9.filtered_ref), custom_call_target="tpu_custom_call" | custom-call | tf_op jit(solution)/shard_map/factor_basis/pallas_call | solution.py:656

commit v4 on v3

--- a/solution.py
+++ b/solution.py
@@ -14,9 +14,9 @@
 CHUNKS = 5
 FIRST = 17 * LANES
 FAR_FIRST = (7, 5, 3, 1, 6, 4, 2)
-NEXT = (1, 4, 2)
-LINE_AFTER = 0
-GATHER_AFTER = 1
+NEXT = (1, 2)
+LINE_AFTER = 1
+GATHER_AFTER = 2
 SPLIT = 4
 GRANT = 16 * 2**20
 MESH = pl.DeviceIdType.MESH
@@ -97,8 +97,8 @@
     first_line_recv,
     first_ag_send,
     first_ag_recv,
-    mate_sem,
-    across_sem,
+    know_sem,
+    all_sem,
     along_sem,
 ):
     space = lax.axis_index("space")
@@ -146,6 +146,11 @@
                 )
 
     tell_line(barrier)
+
+    @pl.when(plane == 0)
+    def _():
+        pl.semaphore_signal(barrier, inc=1, device_id=in_group(4)[1], device_id_type=MESH)
+
     beside = (plane + lines - 1) // lines + (2 * lines - 2 - plane) // lines
 
     own = pl.ds(pl.multiple_of(tm * hours, hours), hours)
@@ -159,7 +164,7 @@
     for copy in (load_x, load_coef, load_own):
         copy.start()
 
-    pl.semaphore_wait(barrier, len(NEXT) + beside)
+    pl.semaphore_wait(barrier, len(NEXT) + beside + (lines - 1 - plane) // (lines - 1))
     swaps = []
     for index, (start, width) in enumerate(spans):
         copy = pltpu.make_async_remote_copy(
@@ -175,13 +180,6 @@
         swaps.append(copy)
     for copy in swaps[:-1]:
         copy.start()
-    pl.semaphore_signal(mate_sem, inc=1, device_id=in_group(2)[1], device_id_type=MESH)
-    pl.semaphore_wait(mate_sem, 1)
-    pl.semaphore_signal(across_sem, inc=1, device_id=in_group(4)[1], device_id_type=MESH)
-    for reach in range(lines - 2):
-        if reach:
-            pl.semaphore_wait(along_sem.at[reach - 1], beside)
-        tell_line(along_sem.at[reach])
 
     load_x.wait()
     for side in range(2):
@@ -210,6 +208,10 @@
     )
     tail_copy.start()
     swaps[-1].start()
+    for reach in range(lines - 2):
+        if reach:
+            pl.semaphore_wait(along_sem.at[reach - 1], beside)
+        tell_line(along_sem.at[reach])
 
     load_coef.wait()
     row = lax.broadcasted_iota(jnp.int32, (total, total), 0)
@@ -268,8 +270,33 @@
                 values, values, (((1,), (1,)), ((), ())), preferred_element_type=jnp.float32
             )
         first_partial[...] = jnp.concatenate([gram[: hours // 2], gram[hours // 2 :]], axis=1)
-        for offset in range(1, PLANE):
-            first_scatter(offset).start()
+
+    def first_stage_scatter():
+        pl.semaphore_wait(along_sem.at[lines - 3], beside)
+
+        @pl.when(plane == 0)
+        def _():
+            for index, k in enumerate((1, 2, 4)):
+                pl.semaphore_signal(
+                    know_sem.at[index],
+                    inc=1,
+                    device_id=in_group(k)[1],
+                    device_id_type=MESH,
+                )
+                pl.semaphore_wait(know_sem.at[index], 1)
+            for offset in range(1, lines):
+                pl.semaphore_signal(
+                    all_sem, inc=1, device_id=in_line(offset), device_id_type=MESH
+                )
+
+        @pl.when(plane > 0)
+        def _():
+            pl.semaphore_wait(all_sem, 1)
+
+        @pl.when(tm == 0)
+        def _():
+            for offset in range(1, PLANE):
+                first_scatter(offset).start()
 
     def first_stage_line():
         @pl.when(tm == 0)
@@ -297,8 +324,6 @@
                     if side or offset:
                         first_gather(offset, side).start()
 
-    pl.semaphore_wait(across_sem, 1)
-    pl.semaphore_wait(along_sem.at[lines - 3], beside)
     load_own.wait()
     partial[...] = jnp.zeros_like(partial)
     for index, (start, width) in enumerate(spans):
@@ -318,6 +343,8 @@
         partial[...] += lax.dot_general(
             values[hours:], values, (((1,), (1,)), ((), ())), preferred_element_type=jnp.float32
         )
+        if index == 0:
+            first_stage_scatter()
         if index == min(LINE_AFTER, len(spans) - 2):
             first_stage_line()
         if index == min(GATHER_AFTER, len(spans) - 2):
@@ -638,7 +665,7 @@
             dma((lines - 1,)),
             dma((group,)),
             dma((PLANE,)),
-            pltpu.SemaphoreType.REGULAR,
+            pltpu.SemaphoreType.REGULAR((3,)),
             pltpu.SemaphoreType.REGULAR,
             pltpu.SemaphoreType.REGULAR((lines - 2,)),
         ],

time: 35.2 us -> 34.8 us (0.989)
  Pallas kernels: 34.4 us -> 34 us
    pallas_call x1, Pallas kernels: 30 us -> 29.6 us  [paired_body(): pl.pallas_call(functools.partial(gather_kernel, swap_spans), out_shape=(j...]
where the time goes in v4:
time: 34.8 us; the launch traced here: 34.6 us
  Pallas kernels  34 us (98%)
  between operations  0.64 us (2%)
    pallas_call x1, Pallas kernels, paired_body(): pl.pallas_call(functools.partial(gather_kernel, swap_spans), out_shape=(j...  29.6 us
    pallas_call x1, Pallas kernels, paired_body(): pl.pallas_call(functools.partial(basis_kernel, points, shift, spans), out...  4.41 us

profile of v4, /device:TPU:0, one launch (start us, length us, event | category | flops | bytes accessed | tf_op | source)
XLA Modules:
  0.0 34.6 jit_solution(5613406680580860175)
XLA Ops:
  0.6 29.6 %gather_gram.1 = (bf16[4480,128]{1,0:T(8,128)(2,1)S(1)}, f32[64,128]{1,0:T(8,128)S(1)}, f32[128,128]{1,0:T(8,128)S(1)}) custom-call(bf16[64,8768]{1,0:T(8,128)(2,1)} %x_hbm.1, f32[1,128]{1,0:T(1,128)} %bitcast.2), custom_call_target="tpu_custom_call" | custom-call | tf_op jit(solution)/shard_map/gather_gram/pallas_call | solution.py:629
  30.2 4.4 %factor_basis.1 = (f32[4384,128]{1,0:T(8,128)}, f32[128,128]{1,0:T(8,128)}) custom-call(f32[64,128]{1,0:T(8,128)S(1)} %get-tuple-element.7.late_ref, f32[128,128]{1,0:T(8,128)S(1)} %get-tuple-element.8.early_ref, bf16[4480,128]{1,0:T(8,128)(2,1)S(1)} %get-tuple-element.9.filtered_ref), custom_call_target="tpu_custom_call" | custom-call | tf_op jit(solution)/shard_map/factor_basis/pallas_call | solution.py:683
